TPU v7x, 32 devices: a whole 2x2x4 slice. The times are simulated.
32 devices in a mesh: tm: 8 (over z, y), stream: 4 (over x, core).
Axes of the slice: x: 2, y: 2, z: 4, core: 2. Of those that a mesh axis runs over, the one named last changes fastest.
Arguments:
- signal: bfloat16 [4, 49152, 256], P('stream', 'tm'), may hold values from -6 to 6
- lengths: int32 [4], P('stream'), may hold values from 12288 to 49152, as said below
- w_conv: bfloat16 [512, 512], replicated, may hold values from -0.25 to 0.25
- w_res: bfloat16 [256, 256], replicated, may hold values from -0.375 to 0.375
- w_in: bfloat16 [256, 1024], replicated, may hold values from -0.375 to 0.375
- w_qkv: bfloat16 [1024, 3072], P(None, 'stream')
- w_out: bfloat16 [1024, 1024], P('stream'), may hold values from -0.1875 to 0.1875
- d_out: bfloat16 [4, 192, 1024], P('stream', 'tm'), may hold values from -6 to 6
Outputs:
- out: bfloat16 [4, 192, 1024], P('stream', 'tm')
- d_signal: bfloat16 [4, 49152, 256], P('stream', 'tm')
- g_conv: float32 [512, 512], P('stream')
- g_res: float32 [256, 256], P('stream')
- g_in: float32 [256, 1024], P('stream')
- g_qkv: float32 [1024, 3072], P('tm', 'stream')
- g_out: float32 [1024, 1024], P('stream', 'tm')
Inputs may be any that keep to these rules, and one draw needn't show every extreme that they name: `lengths`: some stay has all 49152 samples valid and some other stay exactly 12288.
All inputs are finite; a program needn't handle non-finite values.
Results may differ from a plain program's by a relative error of at most 0.013.
Values may be sent and summed in bfloat16 or wider, within the bound.
A program may use at most 128 MiB of HBM per device.

v0:
```python
import math
import jax
import jax.numpy as jnp
from jax import lax
from jax.sharding import PartitionSpec as P

HEADS = 16
POOL = 256
DILATION_STEP = 512
EPS = 1e-05
HIGH = lax.Precision.HIGHEST


def shifted(value, axis, by):
    length = lax.axis_size(axis)
    pairs = [(i, i + by) for i in range(length) if 0 <= i + by < length]
    return lax.ppermute(value, axis, pairs)


def neighbour_rows(block, offset):
    return shifted(block, "tm", offset)


def local(signal, lengths, w_conv, w_res, w_in, w_qkv, w_out, d_out):
    stays, sample_values, chans = signal.shape
    width = w_in.shape[1]
    head_size = width // HEADS
    heads_here = w_out.shape[0] // head_size
    toks_here = sample_values // POOL
    scale = 1.0 / math.sqrt(head_size)
    incoming_rows = neighbour_rows(signal[:, sample_values - DILATION_STEP :], 1)
    past_rows = jnp.concatenate([incoming_rows, signal[:, : sample_values - DILATION_STEP]], axis=1)
    joined = jnp.concatenate([past_rows, signal], axis=2)
    mixed = jnp.einsum("bsc,cd->bsd", joined, w_conv, preferred_element_type=jnp.float32)
    tanh_f = jnp.tanh(mixed[..., :chans])
    sig_g = jax.nn.sigmoid(mixed[..., chans:])
    hidden = (tanh_f * sig_g).astype(jnp.bfloat16)
    sample_pos = lax.axis_index("tm") * sample_values + jnp.arange(sample_values, dtype=jnp.int32)
    valid = (sample_pos[None, :] < lengths[:, None])[..., None]
    resid = jnp.where(
        valid,
        signal.astype(jnp.float32)
        + jnp.einsum("bsc,cd->bsd", hidden, w_res, preferred_element_type=jnp.float32),
        0.0,
    )
    pooled = jnp.mean(resid.reshape(stays, toks_here, POOL, chans), axis=2).astype(jnp.bfloat16)
    own_tok = jnp.einsum("btc,cd->btd", pooled, w_in, preferred_element_type=jnp.float32).astype(
        jnp.bfloat16
    )
    group_tok, group_len = (
        lax.all_gather(own_tok, "stream", axis=0, tiled=True),
        lax.all_gather(lengths, "stream", axis=0, tiled=True),
    )
    tok_values = group_tok.astype(jnp.float32)
    tok_scale = lax.rsqrt(jnp.mean(tok_values * tok_values, axis=-1, keepdims=True) + EPS)
    normed = (tok_values * tok_scale).astype(jnp.bfloat16)
    group = normed.shape[0]
    proj = jnp.einsum("btd,de->bte", normed, w_qkv, preferred_element_type=jnp.float32).astype(
        jnp.bfloat16
    )
    proj = proj.reshape(group, toks_here, heads_here, 3, head_size)
    query = proj[:, :, :, 0]
    keyval = proj[:, :, :, 1:].reshape(group, toks_here, heads_here * 2 * head_size)
    all_kv = lax.all_gather(keyval, "tm", axis=1, tiled=True)
    total = all_kv.shape[1]
    all_kv = all_kv.reshape(group, total, heads_here, 2, head_size)
    keys = all_kv[:, :, :, 0]
    values = all_kv[:, :, :, 1]
    query_pos = lax.axis_index("tm") * toks_here + jnp.arange(toks_here, dtype=jnp.int32)
    key_pos = jnp.arange(total, dtype=jnp.int32)
    allowed = (key_pos[None, None, :] <= query_pos[None, :, None]) & (
        (key_pos * POOL)[None, None, :] < group_len[:, None, None]
    )
    scores = jnp.einsum("bqhe,bkhe->bhqk", query, keys, preferred_element_type=jnp.float32) * scale
    scores = jnp.where(allowed[:, None], scores, -1e30)
    top = jnp.max(scores, axis=-1, keepdims=True)
    weights = jnp.exp(scores - top)
    prob = weights / jnp.sum(weights, axis=-1, keepdims=True)
    prob16 = prob.astype(jnp.bfloat16)
    context = jnp.einsum(
        "bhqk,bkhe->bqhe", prob16, values, preferred_element_type=jnp.float32
    ).astype(jnp.bfloat16)
    context = context.reshape(group, toks_here, heads_here * head_size)
    head_part = jnp.einsum("bte,ed->btd", context, w_out, preferred_element_type=jnp.float32)
    summed = lax.psum_scatter(head_part, "stream", scatter_dimension=0, tiled=True)
    out = (own_tok.astype(jnp.float32) + summed).astype(jnp.bfloat16)
    group_grad = lax.all_gather(d_out, "stream", axis=0, tiled=True)
    g_out_part = jnp.einsum("bte,btd->ed", context, group_grad, preferred_element_type=jnp.float32)
    d_context = jnp.einsum(
        "btd,ed->bte", group_grad, w_out, preferred_element_type=jnp.float32
    ).astype(jnp.bfloat16)
    d_context = d_context.reshape(group, toks_here, heads_here, head_size)
    d_prob = jnp.einsum("bqhe,bkhe->bhqk", d_context, values, preferred_element_type=jnp.float32)
    d_score = prob * (d_prob - jnp.sum(d_prob * prob, axis=-1, keepdims=True))
    d_query = scale * jnp.einsum(
        "bhqk,bkhe->bqhe", d_score, keys.astype(jnp.float32), precision=HIGH
    )
    d_keys = scale * jnp.einsum(
        "bhqk,bqhe->bkhe", d_score, query.astype(jnp.float32), precision=HIGH
    )
    d_values = jnp.einsum("bhqk,bqhe->bkhe", prob16, d_context, preferred_element_type=jnp.float32)
    d_kv = jnp.stack([d_keys, d_values], axis=3).reshape(group, total, heads_here * 2 * head_size)
    d_kv_own = lax.psum_scatter(d_kv, "tm", scatter_dimension=1, tiled=True).reshape(
        group, toks_here, heads_here, 2, head_size
    )
    d_proj = jnp.concatenate([d_query[:, :, :, None], d_kv_own], axis=3).reshape(
        group, toks_here, heads_here * 3 * head_size
    )
    g_qkv_part = jnp.einsum("btd,bte->de", normed.astype(jnp.float32), d_proj, precision=HIGH)
    d_normed = jnp.einsum("bte,de->btd", d_proj, w_qkv.astype(jnp.float32), precision=HIGH)
    inner = jnp.sum(d_normed * tok_values, axis=-1, keepdims=True)
    cube = tok_scale * tok_scale * tok_scale
    d_group = tok_scale * d_normed - tok_values * cube * inner / width
    own_grad = d_out.astype(jnp.float32)
    w_in_wide = w_in.astype(jnp.float32)
    d_tok = lax.psum_scatter(d_group, "stream", scatter_dimension=0, tiled=True) + own_grad
    g_in = jnp.einsum("btc,btd->cd", pooled.astype(jnp.float32), d_tok, precision=HIGH)
    d_pooled = jnp.einsum("btd,cd->btc", d_tok, w_in_wide, precision=HIGH)
    spread = jnp.repeat(d_pooled / POOL, POOL, axis=1)
    d_resid = jnp.where(valid, spread, 0.0).astype(jnp.bfloat16)
    g_res = jnp.einsum("bsc,bsd->cd", hidden, d_resid, preferred_element_type=jnp.float32)
    d_hidden = jnp.einsum("bsd,cd->bsc", d_resid, w_res, preferred_element_type=jnp.float32)
    d_mixed = jnp.concatenate(
        [d_hidden * (1.0 - tanh_f * tanh_f) * sig_g, d_hidden * tanh_f * sig_g * (1.0 - sig_g)],
        axis=2,
    ).astype(jnp.bfloat16)
    g_conv = jnp.einsum("bsc,bsd->cd", joined, d_mixed, preferred_element_type=jnp.float32)
    d_joined = jnp.einsum("bsd,cd->bsc", d_mixed, w_conv, preferred_element_type=jnp.float32)
    past_gradient = d_joined[..., :chans].astype(jnp.bfloat16)
    arriving_rows = neighbour_rows(past_gradient[:, :DILATION_STEP], -1)
    later_gradient = jnp.concatenate([past_gradient[:, DILATION_STEP:], arriving_rows], axis=1)
    d_signal = (
        d_resid.astype(jnp.float32) + d_joined[..., chans:] + later_gradient.astype(jnp.float32)
    ).astype(jnp.bfloat16)
    head_qkv, head_out = (
        lax.psum_scatter(g_qkv_part, "tm", scatter_dimension=0, tiled=True),
        lax.psum_scatter(g_out_part, "tm", scatter_dimension=1, tiled=True),
    )
    sum_conv, sum_res, sum_in = lax.psum((g_conv, g_res, g_in), ("tm", "stream"))
    parts = lax.axis_size("stream")
    index = lax.axis_index("stream")
    conv_rows = sum_conv.shape[0] // parts
    res_rows = sum_res.shape[0] // parts
    in_rows = sum_in.shape[0] // parts
    sum_conv = lax.dynamic_slice_in_dim(sum_conv, index * conv_rows, conv_rows, 0)
    sum_res = lax.dynamic_slice_in_dim(sum_res, index * res_rows, res_rows, 0)
    sum_in = lax.dynamic_slice_in_dim(sum_in, index * in_rows, in_rows, 0)
    return (out, d_signal, sum_conv, sum_res, sum_in, head_qkv, head_out)


def solution(mesh):
    in_specs = (
        P("stream", "tm", None),
        P("stream"),
        P(),
        P(),
        P(),
        P(None, "stream"),
        P("stream", None),
        P("stream", "tm", None),
    )
    out_specs = (
        P("stream", "tm", None),
        P("stream", "tm", None),
        P("stream", None),
        P("stream", None),
        P("stream", None),
        P("tm", "stream"),
        P("stream", "tm"),
    )
    return jax.shard_map(local, mesh=mesh, in_specs=in_specs, out_specs=out_specs, check_vma=False)
```

profile of v0, /device:TPU:0, one launch (start us, length us, event | category | flops | bytes accessed | tf_op | source)
XLA Modules:
  0.0 544.1 jit_solution(6773521519445546995)
XLA Ops:
  8.4 4.9 collective-permute-start
  16.0 4.9 all-reduce
  21.0 5.8 %all_gather.15 = bf16[4,24,1024]{2,1,0:T(8,128)(2,1)S(1)} all-gather(bf16[1,24,1024]{2,1,0:T(8,128)(2,1)} %param.15), channel_id=1, replica_groups=mesh['tm'=8,'stream'=4] {'stream'}, dimensions={0}, use_global_device_ids=true | all-gather | bytes 245760 | tf_op jit(solution)/shard_map/all_gather | solution.py:87
  28.8 3.6 slice.38
  32.5 6.5 %convolution_bitcast_fusion.1 = f32[1,6144,512]{1,2,0:T(8,128)S(1)} fusion(bf16[512,512]{1,0:T(8,128)(2,1)S(1)} %copy-done.17, bf16[1,6144,256]{2,1,0:T(8,128)(2,1)} %param.8, bf16[1,5632,256]{2,1,0:T(8,128)(2,1)} %slice.38, bf16[1,512,256]{2,1,0:T(8,128)(2,1)S(1)} %collective-permute-done), kind=kOutput, calls=%fused_computation.3 | convolution fusion | flops 3240099840 | bytes 19398656 | tf_op jit(solution)/shard_map/bsc,cd->bsd/dot_general | solution.py:34
  41.6 2.8 copy-done.7
  44.4 5.3 fusion.3
  49.7 3.3 reduce_sum.45
  53.2 5.6 %all-gather = bf16[96,1024]{1,0:T(8,128)(2,1)S(1)} all-gather(bf16[24,1024]{1,0:T(8,128)(2,1)S(1)} %convolution_convert_fusion.2), channel_id=2, replica_groups=mesh['tm'=8,'stream'=4] {'stream'}, dimensions={0}, use_global_device_ids=true | all-gather | bytes 245760 | tf_op jit(solution)/shard_map/all_gather | solution.py:51
  60.9 32.5 %all_gather.13 = bf16[4,192,512]{2,0,1:T(4,128)(2,1)S(1)} all-gather(bf16[4,24,512]{2,0,1:T(4,128)(2,1)S(1)} %copy.29), channel_id=1, replica_groups=mesh['tm'=8,'stream'=4] {'tm'}, dimensions={1}, use_global_device_ids=true | all-gather | bytes 884736 | tf_op jit(solution)/shard_map/all_gather | solution.py:64
  96.1 2.8 fusion.59
  105.8 2.8 copy.38
  112.8 83.7 %all-reduce.6.cloned.1.call-done = f32[4,192,512]{2,0,1:T(4,128)} async-done(((f32[4,192,512]{2,0,1:T(4,128)}), f32[4,192,512]{2,0,1:T(4,128)}) %all-reduce.6.cloned.1.call-update) | async-done | bytes 1572880
  208.6 17.2 %reduce-scatter.7.cloned.1.call-done = f32[1,24,1024]{2,1,0:T(8,128)} async-done(((f32[4,24,1024]{2,1,0:T(8,128)}), f32[1,24,1024]{2,1,0:T(8,128)}) %reduce-scatter.7.cloned.1.call-update) | async-done | bytes 98320 | tf_op jit(solution)/shard_map/reduce_scatter | solution.py:116
  230.1 5.9 %fusion.16 = f32[256,256]{1,0:T(8,128)} fusion(bf16[6144,256]{0,1:T(8,128)(2,1)} %copy-done.5, bf16[1,6144,1,1,1,1,256]{6,1,5,4,3,2,0:T(8,128)(2,1)S(1)} %bitcast.125, pred[6144]{0:T(1024)(128)(4,1)S(1)} %add_compare_fusion), kind=kOutput, calls=%fused_computation.31 | convolution fusion | flops 806879232 | bytes 6559744 | tf_op jit(solution)/shard_map/bsc,bsd->cd/dot_general | solution.py:121
  236.1 6.8 %fusion.13 = (bf16[6144,256]{0,1:T(8,128)(2,1)S(1)}, bf16[6144,256]{0,1:T(8,128)(2,1)S(1)}) fusion(f32[1,6144,512]{1,2,0:T(8,128)} %copy-done.7, bf16[6144,256]{1,0:T(8,128)(2,1)S(1)} %fusion.9, bf16[256,256]{1,0:T(8,128)(2,1)S(1)} %copy-done.24), kind=kOutput, calls=%fused_computation.28 | convolution fusion | flops 825753600 | bytes 22151168 | tf_op jit(solution)/shard_map/bsd,cd->bsc/dot_general | solution.py:122
  245.9 4.5 fusion.11
  252.2 3.2 convolution_bitcast_fusion.4
  255.4 10.9 %fusion.60 = (bf16[1,6144,512]{2,1,0:T(8,128)(2,1)S(1)}, f32[1,6144,512]{2,1,0:T(8,128)}) fusion(bf16[512,512]{1,0:T(8,128)(2,1)S(1)} %copy-done.18, bf16[6144,256]{0,1:T(8,128)(2,1)} %copy-done.9, bf16[6144,256]{0,1:T(8,128)(2,1)} %copy-done.8), kind=kOutput, calls=%fused_computation.107 | convolution fusion | flops 3236954112 | bytes 25690112 | tf_op jit(solution)/shard_map/bsd,cd->bsc/dot_general | solution.py:128
  273.8 6.1 %collective-permute-done.1 = bf16[1,512,256]{2,1,0:T(8,128)(2,1)S(1)} collective-permute-done((bf16[1,512,256]{2,1,0:T(8,128)(2,1)S(1)}, bf16[1,512,256]{2,1,0:T(8,128)(2,1)S(1)}, u32[]{:S(2)}, u32[]{:S(2)}) %collective-permute-start.1) | collective-permute-done | bytes 262176 | tf_op jit(solution)/shard_map/ppermute | solution.py:17
  279.9 9.5 %fusion.5 = bf16[1,6144,256]{2,1,0:T(8,128)(2,1)} fusion(f32[1,6144,512]{2,1,0:T(8,128)} %get-tuple-element.19, bf16[1,512,256]{2,1,0:T(8,128)(2,1)S(1)} %collective-permute-done.1, bf16[1,5632,256]{2,1,0:T(8,128)(2,1)S(1)} %slice.55, pred[6144]{0:T(1024)(128)(4,1)S(1)} %add_compare_fusion, bf16[1,6144,256]{2,1,0:T(8,128)(2,1)} %bitcast.126), kind=kLoop, calls=%fused_computation.10 | loop fusion | flops 14155776 | bytes 15734784 | tf_op jit(solution)/shard_map/convert_element_type | solution.py:134
  289.4 103.1 %all-reduce.8.cloned.1.call-done = (f32[512,512]{1,0:T(8,128)}, f32[256,256]{1,0:T(8,128)}, f32[256,1024]{1,0:T(8,128)}) async-done(((f32[512,512]{1,0:T(8,128)}, f32[256,256]{1,0:T(8,128)}, f32[256,1024]{1,0:T(8,128)}), (f32[512,512]{1,0:T(8,128)}, f32[256,256]{1,0:T(8,128)}, f32[256,1024]{1,0:T(8,128)})) %all-reduce.8.cloned.1.call-update) | async-done | bytes 2359312 | tf_op jit(solution)/shard_map/psum | solution.py:139
  397.3 62.8 %reduce-scatter.11.cloned.1.call-done = f32[256,128]{1,0:T(8,128)} async-done(((f32[256,1024]{1,0:T(8,128)}), f32[256,128]{1,0:T(8,128)}) %reduce-scatter.11.cloned.1.call-update) | async-done | bytes 131088 | tf_op jit(solution)/shard_map/reduce_scatter | solution.py:137
  460.1 77.2 %reduce-scatter.9.cloned.1.call-done = f32[128,768]{1,0:T(8,128)} async-done(((f32[1024,768]{1,0:T(8,128)}), f32[128,768]{1,0:T(8,128)}) %reduce-scatter.9.cloned.1.call-update) | async-done | bytes 393232 | tf_op jit(solution)/shard_map/reduce_scatter | solution.py:136
  (129 shorter events, 56.6 us)
Async XLA Ops:
  7.2 52.4 %copy-start = (bf16[1024,768]{1,0:T(8,128)(2,1)S(1)}, bf16[1024,768]{1,0:T(8,128)(2,1)}, u32[]{:S(2)}) copy-start(bf16[1024,768]{1,0:T(8,128)(2,1)} %param.13) | copy-start | bytes 4718596
  7.2 25.3 %copy-start.17 = (bf16[512,512]{1,0:T(8,128)(2,1)S(1)}, bf16[512,512]{1,0:T(8,128)(2,1)}, u32[]{:S(2)}) copy-start(bf16[512,512]{1,0:T(8,128)(2,1)} %param.10) | copy-start | bytes 1572868
  7.2 189.3 %all-reduce.6.cloned.1.call-start = ((), (), s32[]{:S(2)}) async-start(), calls=%async_computation.8 | async-start | bytes 3145728
  8.4 24.1 %collective-permute-start = (bf16[1,512,256]{2,1,0:T(8,128)(2,1)S(1)}, bf16[1,512,256]{2,1,0:T(8,128)(2,1)S(1)}, u32[]{:S(2)}, u32[]{:S(2)}) collective-permute-start(bf16[1,512,256]{2,1,0:T(8,128)(2,1)S(1)} %slice.37), channel_id=1, source_target_pairs={{0,4},{4,8},{8,12},{12,16},{16,20},{20,24},{24,28},{1,5},{5,9},{9,... | collective-permute-start | bytes 786440 | tf_op jit(solution)/shard_map/ppermute | solution.py:17
  32.5 6.5 %copy-start.28 = (bf16[1,512,256]{2,1,0:T(8,128)(2,1)}, bf16[1,512,256]{2,1,0:T(8,128)(2,1)S(1)}, u32[]{:S(2)}) copy-start(bf16[1,512,256]{2,1,0:T(8,128)(2,1)S(1)} %collective-permute-done) | copy-start | bytes 786436
  53.2 6.3 %copy-start.20 = (bf16[24,1024]{1,0:T(8,128)(2,1)}, bf16[24,1024]{1,0:T(8,128)(2,1)S(1)}, u32[]{:S(2)}) copy-start(bf16[24,1024]{1,0:T(8,128)(2,1)S(1)} %convolution_convert_fusion.2) | copy-start | bytes 147460
  59.5 43.4 %copy-start.26 = (f32[4,24]{1,0:T(4,128)}, f32[4,24]{1,0:T(4,128)S(1)}, u32[]{:S(2)}) copy-start(f32[4,24]{1,0:T(4,128)S(1)} %get-tuple-element.13) | copy-start | bytes 1156
  98.9 11.3 %copy-start.25 = (f32[4,4,24]{2,1,0:T(4,128)}, f32[4,4,24]{2,1,0:T(4,128)S(1)}, u32[]{:S(2)}) copy-start(f32[4,4,24]{2,1,0:T(4,128)S(1)} %get-tuple-element.14) | copy-start | bytes 4612
  108.7 117.1 %reduce-scatter.7.cloned.1.call-start = ((), (), s32[]{:S(2)}) async-start(), calls=%async_computation.5 | async-start | bytes 491520 | tf_op jit(solution)/shard_map/reduce_scatter | solution.py:116
  110.2 97.4 %copy-start.11 = (bf16[256,1024]{1,0:T(8,128)(2,1)S(1)}, bf16[256,1024]{1,0:T(8,128)(2,1)}, u32[]{:S(2)}) copy-start(bf16[256,1024]{1,0:T(8,128)(2,1)} %param.14) | copy-start | bytes 1572868
  111.9 113.9 %copy-start.19 = (bf16[1,24,1024]{2,1,0:T(8,128)(2,1)S(1)}, bf16[1,24,1024]{2,1,0:T(8,128)(2,1)}, u32[]{:S(2)}) copy-start(bf16[1,24,1024]{2,1,0:T(8,128)(2,1)} %param.15) | copy-start | bytes 147460
  201.2 24.5 %copy-start.13 = (bf16[256,1024]{1,0:T(8,128)(2,1)S(1)}, bf16[256,1024]{1,0:T(8,128)(2,1)}, u32[]{:S(2)}) copy-start(bf16[256,1024]{1,0:T(8,128)(2,1)} %param.12) | copy-start | bytes 1572868
  205.5 64.7 %reduce-scatter.5.cloned.1.call-start = ((), (), s32[]{:S(2)}) async-start(), calls=%async_computation.4 | async-start | bytes 491520 | tf_op jit(solution)/shard_map/reduce_scatter | solution.py:85
  208.5 184.0 %all-reduce.8.cloned.1.call-start = ((), (), s32[]{:S(2)}) async-start(), calls=%async_computation.9 | async-start | bytes 4718592 | tf_op jit(solution)/shard_map/psum | solution.py:139
  228.2 7.8 %copy-start.24 = (bf16[256,256]{1,0:T(8,128)(2,1)S(1)}, bf16[256,256]{1,0:T(8,128)(2,1)}, u32[]{:S(2)}) copy-start(bf16[256,256]{1,0:T(8,128)(2,1)} %param.11) | copy-start | bytes 393220
  236.1 6.8 %copy-start.22 = (f32[1,24,1024]{2,1,0:T(8,128)S(1)}, f32[1,24,1024]{2,1,0:T(8,128)}, u32[]{:S(2)}) copy-start(f32[1,24,1024]{2,1,0:T(8,128)} %reduce-scatter.7.cloned.1.call-done) | copy-start | bytes 294916
  236.1 9.8 %copy-start.4 = (bf16[1,6144,256]{2,1,0:T(8,128)(2,1)S(1)}, bf16[1,6144,256]{2,1,0:T(8,128)(2,1)}, u32[]{:S(2)}) copy-start(bf16[1,6144,256]{2,1,0:T(8,128)(2,1)} %param.8) | copy-start | bytes 9437188
  236.1 9.8 %copy-start.10 = (bf16[1,5632,256]{2,1,0:T(8,128)(2,1)S(1)}, bf16[1,5632,256]{2,1,0:T(8,128)(2,1)}, u32[]{:S(2)}) copy-start(bf16[1,5632,256]{2,1,0:T(8,128)(2,1)} %slice.38) | copy-start | bytes 8650756
  236.1 9.8 %copy-start.29 = (bf16[1,512,256]{2,1,0:T(8,128)(2,1)S(1)}, bf16[1,512,256]{2,1,0:T(8,128)(2,1)}, u32[]{:S(2)}) copy-start(bf16[1,512,256]{2,1,0:T(8,128)(2,1)} %copy-done.28) | copy-start | bytes 786436
  250.4 209.7 %reduce-scatter.11.cloned.1.call-start = ((), (), s32[]{:S(2)}) async-start(), calls=%async_computation.7 | async-start | bytes 1179648 | tf_op jit(solution)/shard_map/reduce_scatter | solution.py:137
  251.9 285.4 %reduce-scatter.9.cloned.1.call-start = ((), (), s32[]{:S(2)}) async-start(), calls=%async_computation.6 | async-start | bytes 3538944 | tf_op jit(solution)/shard_map/reduce_scatter | solution.py:136
  255.4 14.8 %copy-start.21 = (bf16[24,1024]{1,0:T(8,128)(2,1)S(1)}, bf16[24,1024]{1,0:T(8,128)(2,1)}, u32[]{:S(2)}) copy-start(bf16[24,1024]{1,0:T(8,128)(2,1)} %copy-done.20) | copy-start | bytes 147460
  268.9 11.0 %collective-permute-start.1 = (bf16[1,512,256]{2,1,0:T(8,128)(2,1)S(1)}, bf16[1,512,256]{2,1,0:T(8,128)(2,1)S(1)}, u32[]{:S(2)}, u32[]{:S(2)}) collective-permute-start(bf16[1,512,256]{2,1,0:T(8,128)(2,1)S(1)} %slice.56), channel_id=1, source_target_pairs={{4,0},{8,4},{12,8},{16,12},{20,16},{24,20},{28,24},{5,1},{9,5},{13... | collective-permute-start | bytes 786440 | tf_op jit(solution)/shard_map/ppermute | solution.py:17
  279.9 257.4 %copy-start.1 = (bf16[1024,768]{1,0:T(8,128)(2,1)S(1)}, bf16[1024,768]{1,0:T(8,128)(2,1)}, u32[]{:S(2)}) copy-start(bf16[1024,768]{1,0:T(8,128)(2,1)} %param.13) | copy-start | bytes 4718596
  (15 other events, 62.7 us)
Sparse Core Ops, SparseCore 0:
  108.8 87.6 all-reduce.5
  205.6 20.0 reduce-scatter.6
  228.2 20.8 reduce-scatter.4
  255.4 137.0 all-reduce.7
  396.3 63.7 reduce-scatter.10
  464.1 73.0 reduce-scatter.8
where the time goes:
time: 545 us; the launch traced here: 544 us
  waiting for transfers between devices  350 us (64%)
  matrix products  62.2 us (11%)
  blocking collectives  48.8 us (9%)
  local copies, waits for them, and re-layouts  34.1 us (6%)
  other arithmetic  26.2 us (5%)
  between operations  15.9 us (3%)
  starting transfers between devices  6.85 us (1%)
    psum x1, waiting for transfers between devices, local(): lax.psum((g_conv, g_res, g_in), ('tm', 'stream'))  103 us
    unnamed x7, waiting for transfers between devices  83.8 us
    reduce_scatter x1, waiting for transfers between devices, local(): lax.psum_scatter(g_qkv_part, 'tm', scatter_dimension=0, tiled=True)  77.2 us
    reduce_scatter x1, waiting for transfers between devices, local(): lax.psum_scatter(g_out_part, 'tm', scatter_dimension=1, tiled=True)  62.8 us
    all_gather x1, blocking collectives, local(): all_kv = lax.all_gather(keyval, 'tm', axis=1, tiled=True)  32.5 us
    reduce_scatter x1, waiting for transfers between devices, local(): lax.psum_scatter(d_group, 'stream', scatter_dimension=0, tiled=True)  17.2 us
    unnamed x67, local copies, waits for them, and re-layouts  12.2 us
  transfers between devices with their start and end apart: 8, of which 6 were waited for; matrix products, arithmetic and copies ran while one was open for 13% of the time, Pallas kernels for 0%

commit v1 on v0

--- a/solution.py
+++ b/solution.py
@@ -136,7 +136,7 @@
         lax.psum_scatter(g_qkv_part, "tm", scatter_dimension=0, tiled=True),
         lax.psum_scatter(g_out_part, "tm", scatter_dimension=1, tiled=True),
     )
-    sum_conv, sum_res, sum_in = lax.psum((g_conv, g_res, g_in), ("tm", "stream"))
+    sum_conv, sum_res, sum_in = lax.psum(lax.psum((g_conv, g_res, g_in), "stream"), "tm")
     parts = lax.axis_size("stream")
     index = lax.axis_index("stream")
     conv_rows = sum_conv.shape[0] // parts

time: 545 us -> 594 us (1.090)
  waiting for transfers between devices: 350 us -> 400 us
    psum x1 -> x2, waiting for transfers between devices: 103 us -> 152 us  [the longest x1 97.9 us: local(): lax.psum(lax.psum((g_conv, g_res, g_in), 'stream'), 'tm')]
    unnamed x67 -> x71, local copies, waits for them, and re-layouts: 12.2 us -> 13 us
    unnamed x7 -> x8, waiting for transfers between devices: 83.8 us -> 83.2 us
  transfers between devices with their start and end apart: 8 -> 9, of which waited for: 6 -> 8; matrix products, arithmetic and copies ran while one was open for 13% -> 8% of each run, Pallas kernels for 0% -> 0%
where the time goes in v1:
time: 594 us; the launch traced here: 593 us
  waiting for transfers between devices  400 us (67%)
  matrix products  59 us (10%)
  blocking collectives  48.8 us (8%)
  local copies, waits for them, and re-layouts  36 us (6%)
  other arithmetic  26.5 us (4%)
  between operations  15.9 us (3%)
  starting transfers between devices  6.89 us (1%)
    psum x1, waiting for transfers between devices, local(): lax.psum(lax.psum((g_conv, g_res, g_in), 'stream'), 'tm')  97.9 us
    unnamed x8, waiting for transfers between devices  83.2 us
    reduce_scatter x1, waiting for transfers between devices, local(): lax.psum_scatter(g_qkv_part, 'tm', scatter_dimension=0, tiled=True)  77.5 us
    reduce_scatter x1, waiting for transfers between devices, local(): lax.psum_scatter(g_out_part, 'tm', scatter_dimension=1, tiled=True)  62.9 us
    psum x1, waiting for transfers between devices, local(): lax.psum((g_conv, g_res, g_in), 'stream')  53.8 us
    all_gather x1, blocking collectives, local(): all_kv = lax.all_gather(keyval, 'tm', axis=1, tiled=True)  32.5 us
    reduce_scatter x1, waiting for transfers between devices, local(): lax.psum_scatter(d_group, 'stream', scatter_dimension=0, tiled=True)  20.2 us
    unnamed x71, local copies, waits for them, and re-layouts  13 us
  transfers between devices with their start and end apart: 9, of which 8 were waited for; matrix products, arithmetic and copies ran while one was open for 8% of the time, Pallas kernels for 0%

profile of v1, /device:TPU:0, one launch (start us, length us, event | category | flops | bytes accessed | tf_op | source)
XLA Modules:
  0.0 593.3 jit_solution(3739021843453917341)
XLA Ops:
  8.4 4.9 collective-permute-start
  16.0 4.9 all-reduce
  21.0 5.8 all_gather.15
  28.8 3.6 slice.38
  33.2 6.5 %convolution_bitcast_fusion.1 = f32[1,6144,512]{1,2,0:T(8,128)S(1)} fusion(bf16[512,512]{1,0:T(8,128)(2,1)S(1)} %copy-done.18, bf16[1,6144,256]{2,1,0:T(8,128)(2,1)} %param.8, bf16[1,5632,256]{2,1,0:T(8,128)(2,1)} %slice.38, bf16[1,512,256]{2,1,0:T(8,128)(2,1)S(1)} %collective-permute-done), kind=kOutput, calls=%fused_computation.3 | convolution fusion | flops 3240099840 | bytes 19398656 | tf_op jit(solution)/shard_map/bsc,cd->bsd/dot_general | solution.py:34
  42.2 2.8 copy-done.8
  45.1 5.3 fusion.3
  50.4 3.3 reduce_sum.45
  53.9 5.6 all-gather
  62.2 32.5 %all_gather.13 = bf16[4,192,512]{2,0,1:T(4,128)(2,1)S(1)} all-gather(bf16[4,24,512]{2,0,1:T(4,128)(2,1)S(1)} %copy.29), channel_id=1, replica_groups=mesh['tm'=8,'stream'=4] {'tm'}, dimensions={1}, use_global_device_ids=true | all-gather | bytes 884736 | tf_op jit(solution)/shard_map/all_gather | solution.py:64
  100.3 2.8 convolution_bitcast_fusion.6
  109.1 2.8 copy.38
  116.6 83.0 %all-reduce.8.cloned.1.call-done = f32[4,192,512]{2,0,1:T(4,128)} async-done(((f32[4,192,512]{2,0,1:T(4,128)}), f32[4,192,512]{2,0,1:T(4,128)}) %all-reduce.8.cloned.1.call-update) | async-done | bytes 1572880
  208.6 20.2 %reduce-scatter.7.cloned.1.call-done = f32[1,24,1024]{2,1,0:T(8,128)} async-done(((f32[4,24,1024]{2,1,0:T(8,128)}), f32[1,24,1024]{2,1,0:T(8,128)}) %reduce-scatter.7.cloned.1.call-update) | async-done | bytes 98320 | tf_op jit(solution)/shard_map/reduce_scatter | solution.py:116
  235.2 6.8 %fusion.13 = (bf16[6144,256]{0,1:T(8,128)(2,1)S(1)}, bf16[6144,256]{0,1:T(8,128)(2,1)S(1)}) fusion(f32[1,6144,512]{1,2,0:T(8,128)} %copy-done.8, bf16[6144,256]{1,0:T(8,128)(2,1)S(1)} %fusion.9, bf16[256,256]{1,0:T(8,128)(2,1)S(1)} %copy-done.25), kind=kOutput, calls=%fused_computation.28 | convolution fusion | flops 825753600 | bytes 22151168 | tf_op jit(solution)/shard_map/bsd,cd->bsc/dot_general | solution.py:122
  245.0 4.5 fusion.11
  251.6 53.8 %all-reduce.12.cloned.1.call-done = (f32[512,512]{1,0:T(8,128)}, f32[256,256]{1,0:T(8,128)}, f32[256,1024]{1,0:T(8,128)}) async-done(((f32[512,512]{1,0:T(8,128)}, f32[256,256]{1,0:T(8,128)}, f32[256,1024]{1,0:T(8,128)}), (f32[512,512]{1,0:T(8,128)}, f32[256,256]{1,0:T(8,128)}, f32[256,1024]{1,0:T(8,128)})) %all-reduce.12.cloned.1.call-update) | async-done | bytes 2359312 | tf_op jit(solution)/shard_map/psum | solution.py:139
  307.1 3.2 convolution_bitcast_fusion.4
  310.4 10.9 %fusion.60 = (bf16[1,6144,512]{2,1,0:T(8,128)(2,1)S(1)}, f32[1,6144,512]{2,1,0:T(8,128)}) fusion(bf16[512,512]{1,0:T(8,128)(2,1)S(1)} %copy-done.19, bf16[6144,256]{0,1:T(8,128)(2,1)} %copy-done.10, bf16[6144,256]{0,1:T(8,128)(2,1)} %copy-done.9), kind=kOutput, calls=%fused_computation.107 | convolution fusion | flops 3236954112 | bytes 25690112 | tf_op jit(solution)/shard_map/bsd,cd->bsc/dot_general | solution.py:128
  325.2 3.5 reduce-scatter.5.cloned.1.call-done
  333.5 9.8 %fusion.5 = bf16[1,6144,256]{2,1,0:T(8,128)(2,1)} fusion(f32[1,6144,512]{2,1,0:T(8,128)} %get-tuple-element.22, bf16[1,512,256]{2,1,0:T(8,128)(2,1)S(1)} %collective-permute-done.1, bf16[1,5632,256]{2,1,0:T(8,128)(2,1)S(1)} %slice.55, pred[6144]{0:T(1024)(128)(4,1)S(1)} %add_compare_fusion, bf16[1,6144,256]{2,1,0:T(8,128)(2,1)} %bitcast.126), kind=kLoop, calls=%fused_computation.10 | loop fusion | flops 14155776 | bytes 15734784 | tf_op jit(solution)/shard_map/convert_element_type | solution.py:134
  343.3 97.9 %all-reduce.10.cloned.1.call-done = (f32[512,512]{1,0:T(8,128)}, f32[256,256]{1,0:T(8,128)}, f32[256,1024]{1,0:T(8,128)}) async-done(((f32[512,512]{1,0:T(8,128)}, f32[256,256]{1,0:T(8,128)}, f32[256,1024]{1,0:T(8,128)}), (f32[512,512]{1,0:T(8,128)}, f32[256,256]{1,0:T(8,128)}, f32[256,1024]{1,0:T(8,128)})) %all-reduce.10.cloned.1.call-update) | async-done | bytes 2359312 | tf_op jit(solution)/shard_map/psum | solution.py:139
  446.1 62.9 %reduce-scatter.11.cloned.1.call-done = f32[256,128]{1,0:T(8,128)} async-done(((f32[256,1024]{1,0:T(8,128)}), f32[256,128]{1,0:T(8,128)}) %reduce-scatter.11.cloned.1.call-update) | async-done | bytes 131088 | tf_op jit(solution)/shard_map/reduce_scatter | solution.py:137
  508.9 77.5 %reduce-scatter.9.cloned.1.call-done = f32[128,768]{1,0:T(8,128)} async-done(((f32[1024,768]{1,0:T(8,128)}), f32[128,768]{1,0:T(8,128)}) %reduce-scatter.9.cloned.1.call-update) | async-done | bytes 393232 | tf_op jit(solution)/shard_map/reduce_scatter | solution.py:136
  (136 shorter events, 62.7 us)
Async XLA Ops:
  7.2 53.0 %copy-start = (bf16[1024,768]{1,0:T(8,128)(2,1)S(1)}, bf16[1024,768]{1,0:T(8,128)(2,1)}, u32[]{:S(2)}) copy-start(bf16[1024,768]{1,0:T(8,128)(2,1)} %param.13) | copy-start | bytes 4718596
  7.2 26.0 %copy-start.18 = (bf16[512,512]{1,0:T(8,128)(2,1)S(1)}, bf16[512,512]{1,0:T(8,128)(2,1)}, u32[]{:S(2)}) copy-start(bf16[512,512]{1,0:T(8,128)(2,1)} %param.10) | copy-start | bytes 1572868
  7.2 192.4 %all-reduce.8.cloned.1.call-start = ((), (), s32[]{:S(2)}) async-start(), calls=%async_computation.8 | async-start | bytes 3145728
  8.4 24.8 %collective-permute-start = (bf16[1,512,256]{2,1,0:T(8,128)(2,1)S(1)}, bf16[1,512,256]{2,1,0:T(8,128)(2,1)S(1)}, u32[]{:S(2)}, u32[]{:S(2)}) collective-permute-start(bf16[1,512,256]{2,1,0:T(8,128)(2,1)S(1)} %slice.37), channel_id=1, source_target_pairs={{0,4},{4,8},{8,12},{12,16},{16,20},{20,24},{24,28},{1,5},{5,9},{9,... | collective-permute-start | bytes 786440 | tf_op jit(solution)/shard_map/ppermute | solution.py:17
  60.2 46.0 %copy-start.28 = (f32[4,24]{1,0:T(4,128)}, f32[4,24]{1,0:T(4,128)S(1)}, u32[]{:S(2)}) copy-start(f32[4,24]{1,0:T(4,128)S(1)} %get-tuple-element.16) | copy-start | bytes 1156
  100.3 8.8 %copy-start.26 = (f32[4,4,24]{2,1,0:T(4,128)}, f32[4,4,24]{2,1,0:T(4,128)S(1)}, u32[]{:S(2)}) copy-start(f32[4,4,24]{2,1,0:T(4,128)S(1)} %get-tuple-element.17) | copy-start | bytes 4612
  111.9 116.9 %copy-start.20 = (bf16[1,24,1024]{2,1,0:T(8,128)(2,1)S(1)}, bf16[1,24,1024]{2,1,0:T(8,128)(2,1)}, u32[]{:S(2)}) copy-start(bf16[1,24,1024]{2,1,0:T(8,128)(2,1)} %param.15) | copy-start | bytes 147460
  111.9 116.9 %reduce-scatter.7.cloned.1.call-start = ((), (), s32[]{:S(2)}) async-start(), calls=%async_computation.5 | async-start | bytes 491520 | tf_op jit(solution)/shard_map/reduce_scatter | solution.py:116
  208.6 96.8 %all-reduce.12.cloned.1.call-start = ((), (), s32[]{:S(2)}) async-start(), calls=%async_computation.10 | async-start | bytes 4718592 | tf_op jit(solution)/shard_map/psum | solution.py:139
  235.2 6.8 %copy-start.23 = (f32[1,24,1024]{2,1,0:T(8,128)S(1)}, f32[1,24,1024]{2,1,0:T(8,128)}, u32[]{:S(2)}) copy-start(f32[1,24,1024]{2,1,0:T(8,128)} %reduce-scatter.7.cloned.1.call-done) | copy-start | bytes 294916
  235.2 9.8 %copy-start.4 = (bf16[1,6144,256]{2,1,0:T(8,128)(2,1)S(1)}, bf16[1,6144,256]{2,1,0:T(8,128)(2,1)}, u32[]{:S(2)}) copy-start(bf16[1,6144,256]{2,1,0:T(8,128)(2,1)} %param.8) | copy-start | bytes 9437188
  235.2 9.8 %copy-start.11 = (bf16[1,5632,256]{2,1,0:T(8,128)(2,1)S(1)}, bf16[1,5632,256]{2,1,0:T(8,128)(2,1)}, u32[]{:S(2)}) copy-start(bf16[1,5632,256]{2,1,0:T(8,128)(2,1)} %slice.38) | copy-start | bytes 8650756
  235.2 9.8 %copy-start.32 = (bf16[1,512,256]{2,1,0:T(8,128)(2,1)S(1)}, bf16[1,512,256]{2,1,0:T(8,128)(2,1)}, u32[]{:S(2)}) copy-start(bf16[1,512,256]{2,1,0:T(8,128)(2,1)} %copy-done.31) | copy-start | bytes 786436
  249.5 55.9 %copy-start.17 = (bf16[4,24,1024]{2,1,0:T(8,128)(2,1)S(1)}, bf16[4,24,1024]{2,1,0:T(8,128)(2,1)}, u32[]{:S(2)}) copy-start(bf16[4,24,1024]{2,1,0:T(8,128)(2,1)} %copy-done.16) | copy-start | bytes 589828
  249.5 57.6 %copy-start.15 = (f32[4,24,768]{2,1,0:T(8,128)S(1)}, f32[4,24,768]{2,1,0:T(8,128)}, u32[]{:S(2)}) copy-start(f32[4,24,768]{2,1,0:T(8,128)} %reshape.321) | copy-start | bytes 884740
  249.5 57.6 %copy-start.29 = (f32[4,24]{1,0:T(4,128)S(1)}, f32[4,24]{1,0:T(4,128)}, u32[]{:S(2)}) copy-start(f32[4,24]{1,0:T(4,128)} %copy-done.28) | copy-start | bytes 1156
  249.6 79.1 %reduce-scatter.5.cloned.1.call-start = ((), (), s32[]{:S(2)}) async-start(), calls=%async_computation.4 | async-start | bytes 491520 | tf_op jit(solution)/shard_map/reduce_scatter | solution.py:85
  251.6 58.8 %copy-start.19 = (bf16[512,512]{1,0:T(8,128)(2,1)S(1)}, bf16[512,512]{1,0:T(8,128)(2,1)}, u32[]{:S(2)}) copy-start(bf16[512,512]{1,0:T(8,128)(2,1)} %param.10) | copy-start | bytes 1572868
  251.6 189.7 %all-reduce.10.cloned.1.call-start = ((), (), s32[]{:S(2)}) async-start(), calls=%async_computation.9 | async-start | bytes 4718592 | tf_op jit(solution)/shard_map/psum | solution.py:139
  305.4 203.5 %reduce-scatter.11.cloned.1.call-start = ((), (), s32[]{:S(2)}) async-start(), calls=%async_computation.7 | async-start | bytes 1179648 | tf_op jit(solution)/shard_map/reduce_scatter | solution.py:137
  306.9 279.6 %reduce-scatter.9.cloned.1.call-start = ((), (), s32[]{:S(2)}) async-start(), calls=%async_computation.6 | async-start | bytes 3538944 | tf_op jit(solution)/shard_map/reduce_scatter | solution.py:136
  310.4 18.3 %copy-start.22 = (bf16[24,1024]{1,0:T(8,128)(2,1)S(1)}, bf16[24,1024]{1,0:T(8,128)(2,1)}, u32[]{:S(2)}) copy-start(bf16[24,1024]{1,0:T(8,128)(2,1)} %copy-done.21) | copy-start | bytes 147460
  323.9 9.7 %collective-permute-start.1 = (bf16[1,512,256]{2,1,0:T(8,128)(2,1)S(1)}, bf16[1,512,256]{2,1,0:T(8,128)(2,1)S(1)}, u32[]{:S(2)}, u32[]{:S(2)}) collective-permute-start(bf16[1,512,256]{2,1,0:T(8,128)(2,1)S(1)} %slice.56), channel_id=1, source_target_pairs={{4,0},{8,4},{12,8},{16,12},{20,16},{24,20},{28,24},{5,1},{9,5},{13... | collective-permute-start | bytes 786440 | tf_op jit(solution)/shard_map/ppermute | solution.py:17
  333.5 252.9 %copy-start.1 = (bf16[1024,768]{1,0:T(8,128)(2,1)S(1)}, bf16[1024,768]{1,0:T(8,128)(2,1)}, u32[]{:S(2)}) copy-start(bf16[1024,768]{1,0:T(8,128)(2,1)} %param.13) | copy-start | bytes 4718596
  (18 other events, 75.1 us)
Sparse Core Ops, SparseCore 0:
  112.0 87.5 all-reduce.7
  208.7 20.0 reduce-scatter.6
  249.7 55.6 all-reduce.11
  307.7 20.8 reduce-scatter.4
  332.4 108.7 all-reduce.9
  445.1 63.8 reduce-scatter.10
  513.1 73.2 reduce-scatter.8
